TPU v7x, 512 devices: a whole 4x4x16 slice. The times are simulated.
512 devices in a mesh: dp: 64 (over z_hi, y, x, core), tensor: 8 (over z_lo).
Axes of the slice: x: 4, y: 4, z: 16 (z_hi: 2, z_lo: 8; z = z_hi * 8 + z_lo), core: 2. Of those that a mesh axis runs over, the one named last changes fastest.
Arguments:
- hidden: bfloat16 [8192, 7168], P('dp'), may hold values from -6 to 6
- norm_gain: bfloat16 [7168], replicated, may hold values from 0.099609375 to 1.8984375
- learner_probe_proj: float32 [7168, 4096], P(('dp', 'tensor')), may hold values from -1 to 1
- learner_lookup_proj: float32 [7168, 1024], P(('dp', 'tensor')), may hold values from -3 to 3
- learner_content_proj: float32 [7168, 1024], P(('dp', 'tensor')), may hold values from -0.0625 to 0.0625
- lengths: int32 [4], replicated, may hold values from 1 to 4096, 8192 in all
Outputs:
- serving_combined: bfloat16 [7168, 6144], P('dp', 'tensor')
- spun_lookup_vectors: bfloat16 [8192, 1024], P('dp', 'tensor')
- content_vectors: bfloat16 [8192, 1024], P('dp', 'tensor')
- attention_mix: bfloat16 [8192, 4096], P('dp', 'tensor')
Inputs may be any that keep to these rules, and one draw needn't show every extreme that they name: `lengths`: 4 prompts that fill all 8192 tokens; the longest has exactly 4096 tokens.
All inputs are finite; a program needn't handle non-finite values.
Results may differ from a plain program's by a relative error of at most 0.006.
The roundings to bfloat16 on the way count: a program that leaves them out, or rounds other values in their place, can miss the bound.
Values may be sent and summed in bfloat16 or wider, within the bound.
A program may use at most 64 MiB of HBM per device.

v0:
```python
import math
import jax
import jax.numpy as jnp
from jax import lax
from jax.sharding import PartitionSpec as P

SHARED_KV_NUM = 8
QUARTET_SHARE = 4
PER_ATTN_DIM = 128
rope_theta = 5000000.0
norm_eps = 1e-05
masked_score = -1e30


def document_start(lengths, positions):
    ends = jnp.cumsum(lengths)
    starts = ends - lengths
    inside = (positions[:, None] >= starts[None, :]) & (positions[:, None] < ends[None, :])
    return jnp.sum(jnp.where(inside, starts[None, :], 0), axis=1)


def spin_pairs(content_entries, shift_amounts):
    half_dim = content_entries.shape[-1] // 2
    inverse = rope_theta ** (
        -2.0 * jnp.arange(half_dim, dtype=jnp.float32) / content_entries.shape[-1]
    )
    angles = shift_amounts.astype(jnp.float32)[:, None] * inverse[None, :]
    cosine = jnp.cos(angles)[:, None, :]
    sine = jnp.sin(angles)[:, None, :]
    first = content_entries[..., :half_dim]
    second = content_entries[..., half_dim:]
    return jnp.concatenate(
        [first * cosine - second * sine, second * cosine + first * sine], axis=-1
    )


def per_device(
    hidden, norm_gain, learner_probe_proj, learner_lookup_proj, learner_content_proj, lengths
):
    tok_rows = hidden.shape[0]
    learner_lines = learner_probe_proj.shape[0]
    combined_slab = jnp.concatenate(
        [
            learner_probe_proj.reshape(learner_lines, SHARED_KV_NUM, QUARTET_SHARE * PER_ATTN_DIM),
            learner_lookup_proj.reshape(learner_lines, SHARED_KV_NUM, PER_ATTN_DIM),
            learner_content_proj.reshape(learner_lines, SHARED_KV_NUM, PER_ATTN_DIM),
        ],
        axis=2,
    )
    combined_slab = combined_slab.reshape(
        learner_lines, SHARED_KV_NUM * (QUARTET_SHARE + 2) * PER_ATTN_DIM
    ).astype(jnp.bfloat16)
    serving_combined = lax.all_to_all(
        combined_slab, "tensor", split_axis=1, concat_axis=0, tiled=True
    )
    local_groups = serving_combined.shape[1] // ((QUARTET_SHARE + 2) * PER_ATTN_DIM)
    widened = hidden.astype(jnp.float32)
    scale = lax.rsqrt(jnp.mean(widened * widened, axis=1, keepdims=True) + norm_eps)
    normed = (widened * scale * norm_gain.astype(jnp.float32)[None, :]).astype(jnp.bfloat16)
    mapped_result = jnp.dot(
        normed,
        lax.all_gather(serving_combined, "dp", axis=0, tiled=True),
        preferred_element_type=jnp.float32,
    )
    mapped_result = mapped_result.reshape(tok_rows, local_groups, QUARTET_SHARE + 2, PER_ATTN_DIM)
    query_part = mapped_result[:, :, :QUARTET_SHARE, :]
    key_part = mapped_result[:, :, QUARTET_SHARE, :]
    value_part = mapped_result[:, :, QUARTET_SHARE + 1, :]
    my_index = lax.axis_index("dp") * tok_rows + jnp.arange(tok_rows, dtype=jnp.int32)
    my_start = document_start(lengths, my_index)
    shift_amounts = my_index - my_start
    query_rot = spin_pairs(
        query_part.reshape(tok_rows, local_groups * QUARTET_SHARE, PER_ATTN_DIM), shift_amounts
    ).astype(jnp.bfloat16)
    spun_lookup_vectors = (
        spin_pairs(key_part, shift_amounts)
        .astype(jnp.bfloat16)
        .reshape(tok_rows, local_groups * PER_ATTN_DIM)
    )
    content_vectors = value_part.astype(jnp.bfloat16).reshape(tok_rows, local_groups * PER_ATTN_DIM)
    probe_vectors = query_rot.reshape(
        tok_rows, local_groups, QUARTET_SHARE, PER_ATTN_DIM
    ).transpose(1, 2, 0, 3)
    inv_root = 1.0 / math.sqrt(PER_ATTN_DIM)
    initial = (
        jnp.full((local_groups, QUARTET_SHARE, tok_rows, 1), masked_score, jnp.float32),
        jnp.zeros((local_groups, QUARTET_SHARE, tok_rows, 1), jnp.float32),
        jnp.zeros((local_groups, QUARTET_SHARE, tok_rows, PER_ATTN_DIM), jnp.float32),
    )
    key_piece = lax.all_gather(spun_lookup_vectors, "dp", axis=0, tiled=True)
    value_piece = lax.all_gather(content_vectors, "dp", axis=0, tiled=True)
    span = key_piece.shape[0]
    step_size = math.gcd(span, 512)

    def one_step(turn, state):
        top, total, accum = state
        begin = turn * step_size
        keys_three = lax.dynamic_slice_in_dim(key_piece, begin, step_size, 0).reshape(
            step_size, local_groups, PER_ATTN_DIM
        )
        values_three = lax.dynamic_slice_in_dim(value_piece, begin, step_size, 0).reshape(
            step_size, local_groups, PER_ATTN_DIM
        )
        key_index = begin + jnp.arange(step_size, dtype=jnp.int32)
        key_start = document_start(lengths, key_index)
        allowed = (
            (key_start[None, :] == my_start[:, None])
            & (key_index[None, :] <= my_index[:, None])
            & (key_index[None, :] >= 0)
        )
        scores = (
            jnp.einsum(
                "ghqd,kgd->ghqk", probe_vectors, keys_three, preferred_element_type=jnp.float32
            )
            * inv_root
        )
        scores = jnp.where(allowed, scores, masked_score)
        new_top = jnp.maximum(top, jnp.max(scores, axis=3, keepdims=True))
        weights = jnp.where(allowed, jnp.exp(scores - new_top), 0.0)
        fade = jnp.exp(top - new_top)
        total = total * fade + jnp.sum(weights, axis=3, keepdims=True)
        accum = accum * fade + jnp.einsum(
            "ghqk,kgd->ghqd",
            weights.astype(jnp.bfloat16),
            values_three,
            preferred_element_type=jnp.float32,
        )
        return (new_top, total, accum)

    top, total, accum = lax.fori_loop(0, span // step_size, one_step, initial)
    attention_mix = (
        (accum / total)
        .transpose(2, 0, 1, 3)
        .reshape(tok_rows, local_groups * QUARTET_SHARE * PER_ATTN_DIM)
        .astype(jnp.bfloat16)
    )
    return (serving_combined, spun_lookup_vectors, content_vectors, attention_mix)


def solution(mesh):
    in_specs = (
        P("dp", None),
        P(),
        P(("dp", "tensor"), None),
        P(("dp", "tensor"), None),
        P(("dp", "tensor"), None),
        P(),
    )
    out_specs = (P("dp", "tensor"), P("dp", "tensor"), P("dp", "tensor"), P("dp", "tensor"))
    return jax.shard_map(
        per_device, mesh=mesh, in_specs=in_specs, out_specs=out_specs, check_vma=False
    )
```

profile of v0, /device:TPU:1, one launch (start us, length us, event | category | flops | bytes accessed | tf_op | source)
XLA Modules:
  0.0 520.1 jit_solution(11853927913297743682)
XLA Ops:
  10.2 24.0 %all_to_all.16 = bf16[14,8,768]{2,0,1:T(8,128)(2,1)S(1)} all-to-all(bf16[14,8,768]{2,0,1:T(8,128)(2,1)S(1)} %pad_maximum_fusion), channel_id=1, replica_groups=mesh['dp'=64,'tensor'=8] {'tensor'}, dimensions={1} | all-to-all | bytes 344064 | tf_op jit(solution)/shard_map/all_to_all | solution.py:53
  35.8 195.2 %all-gather.5.cloned.1.call-done = bf16[7168,768]{1,0:T(8,128)(2,1)} async-done(((bf16[112,768]{1,0:T(8,128)(2,1)}), bf16[7168,768]{1,0:T(8,128)(2,1)}) %all-gather.5.cloned.1.call-update) | async-done | bytes 11010064 | tf_op jit(solution)/shard_map/all_gather | solution.py:62
  231.1 7.2 %fusion.23 = f32[128,768]{0,1:T(8,128)S(1)} fusion(bf16[7168,768]{1,0:T(8,128)(2,1)} %all-gather.5.cloned.1.call-done, bf16[128,7168]{1,0:T(8,128)(2,1)S(1)} %copy-done, f32[7168]{0:T(1024)S(1)} %convert_element_type.58, f32[128]{0:T(128)S(1)} %add_rsqrt_fusion), kind=kOutput, calls=%fused_computation.36 | convolution fusion | flops 1412956160 | bytes 13267456 | tf_op jit(solution)/shard_map/dot_general | solution.py:60
  240.1 1.5 copy.38
  242.5 105.7 %all-gather.7.cloned.1.call-done = bf16[8192,128]{0,1:T(8,128)(2,1)} async-done(((bf16[128,128]{0,1:T(8,128)(2,1)}), bf16[8192,128]{0,1:T(8,128)(2,1)}) %all-gather.7.cloned.1.call-update) | async-done | bytes 2097168 | tf_op jit(solution)/shard_map/all_gather | solution.py:90
  348.2 112.0 %all-gather.9.cloned.1.call-done = bf16[8192,1,1,128]{0,3,2,1:T(8,128)(2,1)} async-done(((bf16[128,1,1,128]{0,3,2,1:T(8,128)(2,1)}), bf16[8192,1,1,128]{0,3,2,1:T(8,128)(2,1)}) %all-gather.9.cloned.1.call-update) | async-done | bytes 2097168 | tf_op jit(solution)/shard_map/all_gather | solution.py:91
  460.2 52.4 %while.20 = (s32[]{:T(128)}, f32[1,4,128,1]{2,1,3,0:T(4,128)S(1)}, f32[1,4,128,1]{2,1,3,0:T(4,128)S(1)}, f32[1,4,128,128]{3,2,1,0:T(8,128)S(1)}, s32[1,4]{1,0:T(...) while((s32[]{:T(128)}, f32[1,4,128,1]{2,1,3,0:T(4,128)S(1)}, ...), condition=%wide.region_7.8_spmd.clone, body=%wide.region_3.7_spmd.clone.sunk | while | flops 137050240 | bytes 4371203 | solution.py:130
  462.1 1.3 fusion.53
  465.4 1.3 fusion.53
  468.7 1.3 fusion.53
  472.0 1.3 fusion.53
  475.2 1.3 fusion.53
  478.5 1.3 fusion.53
  480.3 1.2 fusion.50
  481.8 1.3 fusion.53
  485.1 1.3 fusion.53
  488.3 1.3 fusion.53
  491.6 1.3 fusion.53
  494.9 1.3 fusion.53
  498.2 1.3 fusion.53
  501.4 1.3 fusion.53
  504.7 1.3 fusion.53
  508.0 1.3 fusion.53
  511.3 1.3 fusion.53
  (211 shorter events, 36.6 us)
Async XLA Ops:
  7.2 27.9 %copy-start.1 = (bf16[7168]{0:T(1024)(128)(2,1)S(1)}, bf16[7168]{0:T(1024)(128)(2,1)}, u32[]{:S(2)}) copy-start(bf16[7168]{0:T(1024)(128)(2,1)} %param.9) | copy-start | bytes 43012
  7.2 27.9 %copy-start.2 = (s32[4]{0:T(128)S(1)}, s32[4]{0:T(128)}, u32[]{:S(2)}) copy-start(s32[4]{0:T(128)} %param.13) | copy-start | bytes 52
  7.2 28.2 %copy-start = (bf16[128,7168]{1,0:T(8,128)(2,1)S(1)}, bf16[128,7168]{1,0:T(8,128)(2,1)}, u32[]{:S(2)}) copy-start(bf16[128,7168]{1,0:T(8,128)(2,1)} %param.8) | copy-start | bytes 5505028
  7.2 223.9 %all-gather.5.cloned.1.call-start = ((), (), s32[]{:S(2)}) async-start(), calls=%async_computation.1 | async-start | bytes 11182080 | tf_op jit(solution)/shard_map/all_gather | solution.py:62
  35.0 313.2 %all-gather.7.cloned.1.call-start = ((), (), s32[]{:S(2)}) async-start(), calls=%async_computation.2 | async-start | bytes 2129920 | tf_op jit(solution)/shard_map/all_gather | solution.py:90
  239.1 221.1 %all-gather.9.cloned.1.call-start = ((), (), s32[]{:S(2)}) async-start(), calls=%async_computation.3 | async-start | bytes 2129920 | tf_op jit(solution)/shard_map/all_gather | solution.py:91
Sparse Core Ops, SparseCore 0:
  35.1 195.9 all-gather.4
  239.3 108.8 all-gather.6
  352.4 107.7 all-gather.8
where the time goes:
time: 521 us; the launch traced here: 520 us
  waiting for transfers between devices  413 us (79%)
  matrix products  48.6 us (9%)
  blocking collectives  24 us (5%)
  other arithmetic  14.5 us (3%)
  between operations  14 us (3%)
    all_gather x1, waiting for transfers between devices, per_device(): lax.all_gather(serving_combined, 'dp', axis=0, tiled=True)  195 us
    all_gather x1, waiting for transfers between devices, per_device(): value_piece = lax.all_gather(content_vectors, 'dp', axis=0, tiled=True)  112 us
    all_gather x1, waiting for transfers between devices, per_device(): key_piece = lax.all_gather(spun_lookup_vectors, 'dp', axis=0, tiled=True)  106 us
    all_to_all x1, blocking collectives, per_device(): lax.all_to_all(combined_slab, 'tensor', split_axis=1, concat_axis=0, tile...  24 us
    dot_general x16, matrix products, one_step(): jnp.einsum('ghqk,kgd->ghqd', weights.astype(jnp.bfloat16), values_three,...  21.5 us
    dot_general x16, matrix products, one_step(): jnp.einsum('ghqd,kgd->ghqk', probe_vectors, keys_three, preferred_element...  19.9 us
  transfers between devices with their start and end apart: 3, of which 3 were waited for; matrix products, arithmetic and copies ran while one was open for 1% of the time, Pallas kernels for 0%

commit v1 on v0

--- a/solution.py
+++ b/solution.py
@@ -59,7 +59,9 @@
     normed = (widened * scale * norm_gain.astype(jnp.float32)[None, :]).astype(jnp.bfloat16)
     mapped_result = jnp.dot(
         normed,
-        lax.all_gather(serving_combined, "dp", axis=0, tiled=True),
+        jnp.concatenate(
+            lax.all_to_all(jnp.stack([serving_combined] * lax.axis_size("dp")), "dp", 0, 0), axis=0
+        ),
         preferred_element_type=jnp.float32,
     )
     mapped_result = mapped_result.reshape(tok_rows, local_groups, QUARTET_SHARE + 2, PER_ATTN_DIM)

time: 521 us -> 885 us (1.70)
  waiting for transfers between devices: 413 us -> 741 us
  local copies, waits for them, and re-layouts: 4.69 us -> 23.5 us
  starting transfers between devices: 0.12 us -> 17.3 us
    all_gather x1, waiting for transfers between devices: 106 us -> 403 us  [per_device(): key_piece = lax.all_gather(spun_lookup_vectors, 'dp', axis=0, tiled=True)]
    all_to_all x0 -> x1, waiting for transfers between devices: none -> 226 us  [per_device(): lax.all_to_all(jnp.stack([serving_combined] * lax.axis_size('dp')), 'dp',...]
    all_gather x1 -> x0, waiting for transfers between devices: 195 us -> none  [per_device(): lax.all_gather(serving_combined, 'dp', axis=0, tiled=True)]
    all_to_all x0 -> x1, starting transfers between devices: none -> 17.3 us  [per_device(): lax.all_to_all(jnp.stack([serving_combined] * lax.axis_size('dp')), 'dp',...]
    dot_general x0 -> x1, local copies, waits for them, and re-layouts: none -> 14.7 us  [per_device(): jnp.dot(normed, jnp.concatenate(lax.all_to_all(jnp.stack([serving_combine...]
  transfers between devices with their start and end apart: 3 -> 3, of which waited for: 3 -> 3; matrix products, arithmetic and copies ran while one was open for 1% -> 0% of each run, Pallas kernels for 0% -> 0%
where the time goes in v1:
time: 885 us; the launch traced here: 883 us
  waiting for transfers between devices  741 us (84%)
  matrix products  47.4 us (5%)
  blocking collectives  24 us (3%)
  local copies, waits for them, and re-layouts  23.5 us (3%)
  starting transfers between devices  17.3 us (2%)
  other arithmetic  14.3 us (2%)
  between operations  14.3 us (2%)
    all_gather x1, waiting for transfers between devices, per_device(): key_piece = lax.all_gather(spun_lookup_vectors, 'dp', axis=0, tiled=True)  403 us
    all_to_all x1, waiting for transfers between devices, per_device(): lax.all_to_all(jnp.stack([serving_combined] * lax.axis_size('dp')), 'dp',...  226 us
    all_gather x1, waiting for transfers between devices, per_device(): value_piece = lax.all_gather(content_vectors, 'dp', axis=0, tiled=True)  112 us
    all_to_all x1, blocking collectives, per_device(): lax.all_to_all(combined_slab, 'tensor', split_axis=1, concat_axis=0, tile...  24 us
    dot_general x16, matrix products, one_step(): jnp.einsum('ghqk,kgd->ghqd', weights.astype(jnp.bfloat16), values_three,...  21.5 us
    dot_general x16, matrix products, one_step(): jnp.einsum('ghqd,kgd->ghqk', probe_vectors, keys_three, preferred_element...  19.9 us
  transfers between devices with their start and end apart: 3, of which 3 were waited for; matrix products, arithmetic and copies ran while one was open for 0% of the time, Pallas kernels for 0%

profile of v1, /device:TPU:1, one launch (start us, length us, event | category | flops | bytes accessed | tf_op | source)
XLA Modules:
  0.0 883.2 jit_solution(736384294019914806)
XLA Ops:
  10.0 24.0 %all_to_all.21 = bf16[14,8,768]{2,0,1:T(8,128)(2,1)S(1)} all-to-all(bf16[14,8,768]{2,0,1:T(8,128)(2,1)S(1)} %pad_maximum_fusion), channel_id=1, replica_groups=mesh['dp'=64,'tensor'=8] {'tensor'}, dimensions={1} | all-to-all | bytes 344064 | tf_op jit(solution)/shard_map/all_to_all | solution.py:53
  34.1 4.7 stack.2
  38.9 17.3 %all-to-all-start.1 = ((bf16[64,112,768]{2,1,0:T(8,128)(2,1)}), bf16[64,112,768]{2,1,0:T(8,128)(2,1)}, u32[]{:S(2)}, u32[]{:S(2)}) async-start(bf16[64,112,768]{2,1,0:T(8,128)(2,1)} %stack.2), calls=%async_computation.1 | async-start | bytes 22020096 | tf_op jit(solution)/shard_map/all_to_all | solution.py:63
  57.0 226.2 %all-to-all-done.1 = bf16[64,112,768]{2,1,0:T(8,128)(2,1)} async-done(((bf16[64,112,768]{2,1,0:T(8,128)(2,1)}), bf16[64,112,768]{2,1,0:T(8,128)(2,1)}, u32[]{:S(2)}, u32[]{:S(2)}) %all-to-all-start.1) | async-done | bytes 11010080 | tf_op jit(solution)/shard_map/all_to_all | solution.py:63
  283.2 14.7 %copy.36 = bf16[768,7168]{1,0:T(8,128)(2,1)} copy(bf16[768,7168]{0,1:T(8,128)(2,1)} %bitcast.3) | data formatting | bytes 22020096 | tf_op jit(solution)/shard_map/dot_general | solution.py:60
  297.9 5.9 fusion.28
  305.6 1.5 copy.41
  308.1 403.0 %all-gather.4.cloned.1.call-done = bf16[8192,128]{0,1:T(8,128)(2,1)} async-done(((bf16[128,128]{0,1:T(8,128)(2,1)}), bf16[8192,128]{0,1:T(8,128)(2,1)}) %all-gather.4.cloned.1.call-update) | async-done | bytes 2097168 | tf_op jit(solution)/shard_map/all_gather | solution.py:92
  711.0 112.0 %all-gather.6.cloned.1.call-done = bf16[8192,1,1,128]{0,3,2,1:T(8,128)(2,1)} async-done(((bf16[128,1,1,128]{0,3,2,1:T(8,128)(2,1)}), bf16[8192,1,1,128]{0,3,2,1:T(8,128)(2,1)}) %all-gather.6.cloned.1.call-update) | async-done | bytes 2097168 | tf_op jit(solution)/shard_map/all_gather | solution.py:93
  823.1 52.4 %while.20 = (s32[]{:T(128)}, f32[1,4,128,1]{2,1,3,0:T(4,128)S(1)}, f32[1,4,128,1]{2,1,3,0:T(4,128)S(1)}, f32[1,4,128,128]{3,2,1,0:T(8,128)S(1)}, s32[1,4]{1,0:T(...) while((s32[]{:T(128)}, f32[1,4,128,1]{2,1,3,0:T(4,128)S(1)}, ...), condition=%wide.region_7.8_spmd.clone, body=%wide.region_3.7_spmd.clone.sunk | while | flops 137050240 | bytes 4371203 | solution.py:132
  824.9 1.3 fusion.57
  828.2 1.3 fusion.57
  831.5 1.3 fusion.57
  834.8 1.3 fusion.57
  838.1 1.3 fusion.57
  841.3 1.3 fusion.57
  844.6 1.3 fusion.57
  847.9 1.3 fusion.57
  851.2 1.3 fusion.57
  854.4 1.3 fusion.57
  861.0 1.3 fusion.57
  864.3 1.3 fusion.57
  867.6 1.3 fusion.57
  870.8 1.3 fusion.57
  (214 shorter events, 39.7 us)
Async XLA Ops:
  34.1 4.8 copy-start.1
  38.9 17.3 %copy-start.2 = (bf16[7168]{0:T(1024)(128)(2,1)S(1)}, bf16[7168]{0:T(1024)(128)(2,1)}, u32[]{:S(2)}) copy-start(bf16[7168]{0:T(1024)(128)(2,1)} %param.9) | copy-start | bytes 43012
  38.9 17.4 %copy-start.3 = (s32[4]{0:T(128)S(1)}, s32[4]{0:T(128)}, u32[]{:S(2)}) copy-start(s32[4]{0:T(128)} %param.13) | copy-start | bytes 52
  38.9 17.7 %copy-start = (bf16[128,7168]{1,0:T(8,128)(2,1)S(1)}, bf16[128,7168]{1,0:T(8,128)(2,1)}, u32[]{:S(2)}) copy-start(bf16[128,7168]{1,0:T(8,128)(2,1)} %param.8) | copy-start | bytes 5505028
  38.9 244.3 %all-to-all-start.1 = ((bf16[64,112,768]{2,1,0:T(8,128)(2,1)}), bf16[64,112,768]{2,1,0:T(8,128)(2,1)}, u32[]{:S(2)}, u32[]{:S(2)}) async-start(bf16[64,112,768]{2,1,0:T(8,128)(2,1)} %stack.2), calls=%async_computation.1 | async-start | bytes 22020096 | tf_op jit(solution)/shard_map/all_to_all | solution.py:63
  56.1 654.9 %all-gather.4.cloned.1.call-start = ((), (), s32[]{:S(2)}) async-start(), calls=%async_computation.2 | async-start | bytes 2129920 | tf_op jit(solution)/shard_map/all_gather | solution.py:92
  304.7 518.4 %all-gather.6.cloned.1.call-start = ((), (), s32[]{:S(2)}) async-start(), calls=%async_computation.3 | async-start | bytes 2129920 | tf_op jit(solution)/shard_map/all_gather | solution.py:93
Sparse Core Ops, SparseCore 0:
  304.8 406.2 all-gather.3
  715.2 107.7 all-gather.5
